TPU v7x, 32 devices: a whole 2x2x4 slice. The times are simulated.
32 devices in a mesh: groups: 2 (over y), theta: 16 (over z, x, core).
Axes of the slice: x: 2, y: 2, z: 4, core: 2. Of those that a mesh axis runs over, the one named last changes fastest.
Arguments:
- state_now: float32 [5, 2, 64, 256, 128], P(None, None, 'theta', 'groups'), parts along dimension 3, may hold values from -6 to 6
- state_prev: float32 [5, 2, 64, 256, 128], P(None, None, 'theta', 'groups'), parts along dimension 3, may hold values from -6 to 6
- eddy_visc: float32 [2, 64, 256, 128], P(None, 'theta', 'groups'), parts along dimension 2, may hold values from 0.01 to 0.2
- mean_flow: float32 [2, 4], replicated, may hold values from 0.5 to 1
- offset: int32 [2], P('groups'), parts along dimension 0, may hold values from 0 to 63
Outputs:
- field: float32 [5, 2, 64, 256, 128], P(None, None, 'theta', 'groups'), parts along dimension 3
There are 2 independent parts, one for each index of `groups`. A program takes and returns all parts, laid end to end along the dimension named above; an argument that names none is the same for every part. Nothing has to cross between parts.
All inputs are finite; a program needn't handle non-finite values.
Results may differ from a plain program's by a relative error of at most 0.00002.
Values sent between devices are 32-bit elements; how exact they have to be, the bound alone decides.
A program may use at most 128 MiB of HBM per device.

v0:
```python
import jax
import jax.numpy as jnp
from jax import lax
from jax.sharding import PartitionSpec as P

ITERS = 2


PSEUDO_STEP = 0.2
PHYS_STEP = 1.0
SECTION_WEIGHTS = (0.6, 0.6, 1.0)


def with_halo(cells, sides, width):
    for axis, dim in sides:
        count = lax.axis_size(axis)
        head = lax.slice_in_dim(cells, 0, width, axis=dim)
        tail = lax.slice_in_dim(cells, cells.shape[dim] - width, cells.shape[dim], axis=dim)
        cells = jnp.concatenate(
            [
                lax.ppermute(tail, axis, [(i, (i + 1) % count) for i in range(count)]),
                cells,
                lax.ppermute(head, axis, [((i + 1) % count, i) for i in range(count)]),
            ],
            axis=dim,
        )
    return cells


def from_behind(value, axis, steps):
    count = lax.axis_size(axis)
    pairs = [(source, (source + steps) % count) for source in range(count)]
    return lax.ppermute(value, axis, pairs)


def operator_terms(padded, low_ghost, high_ghost, mean_row, eddy_row):
    center = padded[:, 1:-1]
    theta_diff = (padded[:, 2:] - padded[:, :-2]) * 0.5
    neighbours = padded[:, 2:] + padded[:, :-2]
    wall_sign = jnp.array([1.0, 1.0, 1.0, -1.0, 1.0], jnp.float32).reshape(5, 1, 1, 1)
    radial_pad = jnp.concatenate(
        [center[:, :, :1] * wall_sign, center, center[:, :, -1:] * wall_sign], axis=2
    )
    radial_diff = (radial_pad[:, :, 2:] - radial_pad[:, :, :-2]) * 0.5
    neighbours = neighbours + radial_pad[:, :, 2:] + radial_pad[:, :, :-2]
    axial_pad = jnp.concatenate([low_ghost[..., None], center, high_ghost[..., None]], axis=3)
    axial_diff = (axial_pad[..., 2:] - axial_pad[..., :-2]) * 0.5
    neighbours = neighbours + axial_pad[..., 2:] + axial_pad[..., :-2]
    laplace = neighbours - 6.0 * center
    axial_speed = mean_row[0]
    swirl_speed = mean_row[1]
    density = mean_row[2]
    sound_speed = mean_row[3]
    convect = axial_speed * axial_diff + swirl_speed * theta_diff
    divergence = axial_diff[1] + theta_diff[2] + radial_diff[3]
    pressure_push = jnp.stack(
        [
            density * divergence,
            axial_diff[4] / density,
            theta_diff[4] / density,
            radial_diff[4] / density,
            density * sound_speed * sound_speed * divergence,
        ]
    )
    return convect + pressure_push - eddy_row * laplace


def widen(field):
    rotor_pad = with_halo(field[:, 0], (("theta", 1),), 1)
    stator_pad = with_halo(field[:, 1], (("theta", 1),), 1)
    return (rotor_pad, stator_pad)


def paired_planes(rotor_plane, stator_plane, shift_cells):
    cells = rotor_plane.shape[1]
    axis_count = lax.axis_size("theta")
    sectors = shift_cells // cells
    within = shift_cells % cells
    amounts = (
        jnp.stack([sectors, sectors + 1, axis_count - sectors, axis_count - sectors - 1])
        % axis_count
    )
    stacked = jnp.stack([rotor_plane, rotor_plane, stator_plane, stator_plane])
    levels = axis_count.bit_length() - 1
    for level in range(levels):
        moved = from_behind(stacked, "theta", 1 << level)
        taken = amounts >> level & 1 == 1
        stacked = jnp.where(taken[:, None, None, None], moved, stacked)
    stator_low = lax.dynamic_slice_in_dim(
        jnp.concatenate([stacked[1], stacked[0]], axis=1), cells - within, cells, 1
    )
    rotor_high = lax.dynamic_slice_in_dim(
        jnp.concatenate([stacked[2], stacked[3]], axis=1), within, cells, 1
    )
    return (rotor_high, stator_low)


def per_device(state_now, state_prev, eddy_visc, mean_flow, offset):
    cells = state_now.shape[2]
    shift_cells = offset[0] % (cells * lax.axis_size("theta"))
    fixed_part = (state_prev - 4.0 * state_now) * (0.5 / PHYS_STEP)
    field = state_now
    for sweep in range(ITERS):
        start_field = field
        for weight in SECTION_WEIGHTS:
            rotor_pad, stator_pad = widen(field)
            rotor_high, stator_low = paired_planes(
                field[:, 0, :, :, -1], field[:, 1, :, :, 0], shift_cells
            )
            rotor_terms = operator_terms(
                rotor_pad, jnp.zeros_like(rotor_high), rotor_high, mean_flow[0], eddy_visc[0]
            )
            stator_terms = operator_terms(
                stator_pad, stator_low, field[:, 1, :, :, -1], mean_flow[1], eddy_visc[1]
            )
            terms = jnp.stack([rotor_terms, stator_terms], axis=1)
            field = start_field - weight * PSEUDO_STEP * (
                terms + 1.5 / PHYS_STEP * field + fixed_part
            )
    return field


def solution(mesh):
    placed = (
        P(None, None, "theta", "groups", None),
        P(None, None, "theta", "groups", None),
        P(None, "theta", "groups", None),
        P(),
        P("groups"),
    )
    return jax.shard_map(
        per_device,
        mesh=mesh,
        in_specs=placed,
        out_specs=P(None, None, "theta", "groups", None),
        check_vma=False,
    )
```

profile of v0, /device:TPU:0, one launch (start us, length us, event | category | flops | bytes accessed | tf_op | source)
XLA Modules:
  0.0 372.0 jit_solution(15294861376039923022)
XLA Ops:
  18.4 6.5 %slice_multiply_fusion.22 = (f32[5,4,1,128]{2,1,0,3:T(4,128)}, f32[5,4,1,128]{2,1,0,3:T(4,128)}, f32[5,4,1,128]{2,1,0,3:T(4,128)}, f32[5,4,1,128]{2,1,0,3:T(4,128)}) fusion(f32[5,4,128,128]{2,1,0,3:T(4,128)} %copy-done.3, f32[5]{0:T(128)S(1)} %copy-done.10, f32[5,4,128,128]{2,1,0,3:T(4,128)} %copy-done.1), kind=kLoop, calls=%fused_computation.126 | loop fusion | flops 10240 | bytes 81940 | tf_op jit(solution)/shard_map/mul | solution.py:42
  26.1 5.0 %collective-permute-done.2 = f32[4,5,4,128]{3,2,1,0:T(4,128)S(1)} collective-permute-done((f32[4,5,4,128]{3,2,1,0:T(4,128)S(1)}, f32[4,5,4,128]{3,2,1,0:T(4,128)S(1)}, u32[]{:S(2)}, u32[]{:S(2)}) %collective-permute-start.2) | collective-permute-done | bytes 40992 | tf_op jit(solution)/shard_map/ppermute | solution.py:33
  44.9 9.3 %fusion.31 = (f32[5,4,128,128]{2,1,0,3:T(4,128)S(1)}, f32[5,4,128,128]{2,1,0,3:T(4,128)S(1)}, f32[5,4,128,128]{2,1,0,3:T(4,128)S(1)}) fusion(f32[5,4,128,1]{2,1,0,3:T(4,128)S(1)} %get-tuple-element.35, f32[5,4,128,128]{2,1,0,3:T(4,128)} %copy-done.1, f32[5,4,128,1]{2,1,0,3:T(4,128)S(1)} %get-tuple-element.170, ...), kind=kLoop, calls=%fused_computation.170 | loop fusion | flops 3932160 | bytes 5939200 | tf_op jit(solution)/shard_map/mul | solution.py:47
  57.4 5.5 %fusion.29 = (f32[5,4,128,128]{2,1,0,3:T(4,128)S(1)}, f32[5,4,128,128]{2,1,0,3:T(4,128)S(1)}, f32[5,4,128,128]{2,1,0,3:T(4,128)S(1)}) fusion(f32[5,4,128,128]{2,1,0,3:T(4,128)S(1)} %copy-done.4, f32[5,4,128,1]{2,1,0,3:T(4,128)S(1)} %get-tuple-element.171, f32[5,1,128,128]{2,1,0,3:T(1,128)} %collective-permute-done.5, ...), kind=kLoop, calls=%fused_computation.168 | loop fusion | flops 3604480 | bytes 5928960 | tf_op jit(solution)/shard_map/mul | solution.py:47
  67.0 5.8 %subtract_bitcast_fusion.10 = f32[5,1,4,128,128]{3,2,0,4,1:T(4,128)S(1)} fusion(f32[5,4,128,128]{2,1,0,3:T(4,128)S(1)} %copy-done.2, f32[5,4,128,128]{2,1,0,3:T(4,128)S(1)} %multiply_dynamic-update-slice_fusion.20, f32[5,4,128,1]{2,1,0,3:T(4,128)S(1)} %get-tuple-element.35, f32[5,4,128,1]{2,1,0,3:T(4,128)S(1)} %get-tuple-element.170, ...), kind=kLoop, calls=%fused_computation.153 | loop fusion | flops 6881280 | bytes 4890632 | tf_op jit(solution)/shard_map/stack | solution.py:116
  72.9 5.9 %subtract_bitcast_fusion.11 = f32[5,1,4,128,128]{3,2,0,4,1:T(4,128)S(1)} fusion(f32[5,4,128,128]{2,1,0,3:T(4,128)S(1)} %copy-done.4, f32[5,4,128,128]{2,1,0,3:T(4,128)S(1)} %multiply_dynamic-update-slice_fusion.22, f32[5,4,128,1]{2,1,0,3:T(4,128)S(1)} %get-tuple-element.171, f32[5,1,128,128]{2,1,0,3:T(1,128)} %collective-permute-done.4, ...), kind=kLoop, calls=%fused_computation.155 | loop fusion | flops 6553600 | bytes 4880392 | tf_op jit(solution)/shard_map/stack | solution.py:116
  81.5 5.7 %collective-permute-done.8 = f32[4,5,4,128]{3,2,1,0:T(4,128)S(1)} collective-permute-done((f32[4,5,4,128]{3,2,1,0:T(4,128)S(1)}, f32[4,5,4,128]{3,2,1,0:T(4,128)S(1)}, u32[]{:S(2)}, u32[]{:S(2)}) %collective-permute-start.8) | collective-permute-done | bytes 40992 | tf_op jit(solution)/shard_map/ppermute | solution.py:33
  88.9 5.0 %collective-permute-done.9 = f32[4,5,4,128]{3,2,1,0:T(4,128)S(1)} collective-permute-done((f32[4,5,4,128]{3,2,1,0:T(4,128)S(1)}, f32[4,5,4,128]{3,2,1,0:T(4,128)S(1)}, u32[]{:S(2)}, u32[]{:S(2)}) %collective-permute-start.9) | collective-permute-done | bytes 40992 | tf_op jit(solution)/shard_map/ppermute | solution.py:33
  94.5 5.3 %collective-permute-done.10 = f32[4,5,4,128]{3,2,1,0:T(4,128)S(1)} collective-permute-done((f32[4,5,4,128]{3,2,1,0:T(4,128)S(1)}, f32[4,5,4,128]{3,2,1,0:T(4,128)S(1)}, u32[]{:S(2)}, u32[]{:S(2)}) %collective-permute-start.10) | collective-permute-done | bytes 40992 | tf_op jit(solution)/shard_map/ppermute | solution.py:33
  109.8 5.1 %fusion.33 = (f32[5,4,128,128]{2,1,0,3:T(4,128)S(1)}, f32[5,4,128,128]{2,1,0,3:T(4,128)S(1)}, f32[5,4,128,128]{2,1,0,3:T(4,128)S(1)}) fusion(f32[5,4,128,1]{2,1,0,3:T(4,128)S(1)} %get-tuple-element.30, f32[5,4,128,128]{2,1,0,3:T(4,128)S(1)} %get-tuple-element.28, f32[5,4,128,1]{2,1,0,3:T(4,128)S(1)} %fusion.83, ...), kind=kLoop, calls=%fused_computation.172 | loop fusion | flops 3932160 | bytes 5939200 | tf_op jit(solution)/shard_map/mul | solution.py:47
  125.7 4.9 %subtract_bitcast_fusion.8 = f32[5,1,4,128,128]{3,2,0,4,1:T(4,128)S(1)} fusion(f32[5,4,128,128]{2,1,0,3:T(4,128)S(1)} %get-tuple-element.28, f32[5,4,128,128]{2,1,0,3:T(4,128)S(1)} %multiply_dynamic-update-slice_fusion.16, f32[5,4,128,1]{2,1,0,3:T(4,128)S(1)} %get-tuple-element.30, f32[5,4,128,1]{2,1,0,3:T(4,128)S(1)} %fusion.83, ...), kind=kLoop, calls=%fused_computation.149 | loop fusion | flops 6881280 | bytes 4890632 | tf_op jit(solution)/shard_map/stack | solution.py:116
  138.7 5.7 %collective-permute-done.16 = f32[4,5,4,128]{3,2,1,0:T(4,128)S(1)} collective-permute-done((f32[4,5,4,128]{3,2,1,0:T(4,128)S(1)}, f32[4,5,4,128]{3,2,1,0:T(4,128)S(1)}, u32[]{:S(2)}, u32[]{:S(2)}) %collective-permute-start.16) | collective-permute-done | bytes 40992 | tf_op jit(solution)/shard_map/ppermute | solution.py:33
  146.3 5.0 %collective-permute-done.17 = f32[4,5,4,128]{3,2,1,0:T(4,128)S(1)} collective-permute-done((f32[4,5,4,128]{3,2,1,0:T(4,128)S(1)}, f32[4,5,4,128]{3,2,1,0:T(4,128)S(1)}, u32[]{:S(2)}, u32[]{:S(2)}) %collective-permute-start.17) | collective-permute-done | bytes 40992 | tf_op jit(solution)/shard_map/ppermute | solution.py:33
  151.9 5.3 %collective-permute-done.18 = f32[4,5,4,128]{3,2,1,0:T(4,128)S(1)} collective-permute-done((f32[4,5,4,128]{3,2,1,0:T(4,128)S(1)}, f32[4,5,4,128]{3,2,1,0:T(4,128)S(1)}, u32[]{:S(2)}, u32[]{:S(2)}) %collective-permute-start.18) | collective-permute-done | bytes 40992 | tf_op jit(solution)/shard_map/ppermute | solution.py:33
  167.2 5.1 %fusion.35 = (f32[5,4,128,128]{2,1,0,3:T(4,128)S(1)}, f32[5,4,128,128]{2,1,0,3:T(4,128)S(1)}, f32[5,4,128,128]{2,1,0,3:T(4,128)S(1)}) fusion(f32[5,4,128,1]{2,1,0,3:T(4,128)S(1)} %get-tuple-element.25, f32[5,4,128,128]{2,1,0,3:T(4,128)S(1)} %get-tuple-element.23, f32[5,4,128,1]{2,1,0,3:T(4,128)S(1)} %fusion.79, ...), kind=kLoop, calls=%fused_computation.174 | loop fusion | flops 3932160 | bytes 5939200 | tf_op jit(solution)/shard_map/mul | solution.py:47
  183.1 4.9 %subtract_bitcast_fusion.6 = f32[5,1,4,128,128]{3,2,0,4,1:T(4,128)S(1)} fusion(f32[5,4,128,128]{2,1,0,3:T(4,128)S(1)} %get-tuple-element.23, f32[5,4,128,128]{2,1,0,3:T(4,128)S(1)} %multiply_dynamic-update-slice_fusion.12, f32[5,4,128,1]{2,1,0,3:T(4,128)S(1)} %get-tuple-element.25, f32[5,4,128,1]{2,1,0,3:T(4,128)S(1)} %fusion.79, ...), kind=kLoop, calls=%fused_computation.145 | loop fusion | flops 6881280 | bytes 4890632 | tf_op jit(solution)/shard_map/stack | solution.py:116
  195.5 5.7 %collective-permute-done.24 = f32[4,5,4,128]{3,2,1,0:T(4,128)S(1)} collective-permute-done((f32[4,5,4,128]{3,2,1,0:T(4,128)S(1)}, f32[4,5,4,128]{3,2,1,0:T(4,128)S(1)}, u32[]{:S(2)}, u32[]{:S(2)}) %collective-permute-start.24) | collective-permute-done | bytes 40992 | tf_op jit(solution)/shard_map/ppermute | solution.py:33
  203.3 5.0 %collective-permute-done.25 = f32[4,5,4,128]{3,2,1,0:T(4,128)S(1)} collective-permute-done((f32[4,5,4,128]{3,2,1,0:T(4,128)S(1)}, f32[4,5,4,128]{3,2,1,0:T(4,128)S(1)}, u32[]{:S(2)}, u32[]{:S(2)}) %collective-permute-start.25) | collective-permute-done | bytes 40992 | tf_op jit(solution)/shard_map/ppermute | solution.py:33
  209.0 5.3 %collective-permute-done.26 = f32[4,5,4,128]{3,2,1,0:T(4,128)S(1)} collective-permute-done((f32[4,5,4,128]{3,2,1,0:T(4,128)S(1)}, f32[4,5,4,128]{3,2,1,0:T(4,128)S(1)}, u32[]{:S(2)}, u32[]{:S(2)}) %collective-permute-start.26) | collective-permute-done | bytes 40992 | tf_op jit(solution)/shard_map/ppermute | solution.py:33
  224.2 5.1 %fusion.37 = (f32[5,4,128,128]{2,1,0,3:T(4,128)S(1)}, f32[5,4,128,128]{2,1,0,3:T(4,128)S(1)}, f32[5,4,128,128]{2,1,0,3:T(4,128)S(1)}) fusion(f32[5,4,128,1]{2,1,0,3:T(4,128)S(1)} %get-tuple-element.20, f32[5,4,128,128]{2,1,0,3:T(4,128)S(1)} %get-tuple-element.18, f32[5,4,128,1]{2,1,0,3:T(4,128)S(1)} %fusion.75, ...), kind=kLoop, calls=%fused_computation.176 | loop fusion | flops 3932160 | bytes 5939200 | tf_op jit(solution)/shard_map/mul | solution.py:47
  240.2 4.9 %subtract_bitcast_fusion.4 = f32[5,1,4,128,128]{3,2,0,4,1:T(4,128)S(1)} fusion(f32[5,4,128,128]{2,1,0,3:T(4,128)S(1)} %get-tuple-element.18, f32[5,4,128,128]{2,1,0,3:T(4,128)S(1)} %multiply_dynamic-update-slice_fusion.8, f32[5,4,128,1]{2,1,0,3:T(4,128)S(1)} %get-tuple-element.20, f32[5,4,128,1]{2,1,0,3:T(4,128)S(1)} %fusion.75, ...), kind=kLoop, calls=%fused_computation.141 | loop fusion | flops 6881280 | bytes 4890632 | tf_op jit(solution)/shard_map/stack | solution.py:116
  252.5 5.7 %collective-permute-done.32 = f32[4,5,4,128]{3,2,1,0:T(4,128)S(1)} collective-permute-done((f32[4,5,4,128]{3,2,1,0:T(4,128)S(1)}, f32[4,5,4,128]{3,2,1,0:T(4,128)S(1)}, u32[]{:S(2)}, u32[]{:S(2)}) %collective-permute-start.32) | collective-permute-done | bytes 40992 | tf_op jit(solution)/shard_map/ppermute | solution.py:33
  260.1 5.0 %collective-permute-done.33 = f32[4,5,4,128]{3,2,1,0:T(4,128)S(1)} collective-permute-done((f32[4,5,4,128]{3,2,1,0:T(4,128)S(1)}, f32[4,5,4,128]{3,2,1,0:T(4,128)S(1)}, u32[]{:S(2)}, u32[]{:S(2)}) %collective-permute-start.33) | collective-permute-done | bytes 40992 | tf_op jit(solution)/shard_map/ppermute | solution.py:33
  265.8 5.3 %collective-permute-done.34 = f32[4,5,4,128]{3,2,1,0:T(4,128)S(1)} collective-permute-done((f32[4,5,4,128]{3,2,1,0:T(4,128)S(1)}, f32[4,5,4,128]{3,2,1,0:T(4,128)S(1)}, u32[]{:S(2)}, u32[]{:S(2)}) %collective-permute-start.34) | collective-permute-done | bytes 40992 | tf_op jit(solution)/shard_map/ppermute | solution.py:33
  281.0 5.1 %fusion.39 = (f32[5,4,128,128]{2,1,0,3:T(4,128)S(1)}, f32[5,4,128,128]{2,1,0,3:T(4,128)S(1)}, f32[5,4,128,128]{2,1,0,3:T(4,128)S(1)}) fusion(f32[5,4,128,1]{2,1,0,3:T(4,128)S(1)} %get-tuple-element.15, f32[5,4,128,128]{2,1,0,3:T(4,128)S(1)} %get-tuple-element.13, f32[5,4,128,1]{2,1,0,3:T(4,128)S(1)} %fusion.71, ...), kind=kLoop, calls=%fused_computation.178 | loop fusion | flops 3932160 | bytes 5939200 | tf_op jit(solution)/shard_map/mul | solution.py:47
  297.0 4.9 %subtract_bitcast_fusion.2 = f32[5,1,4,128,128]{3,2,0,4,1:T(4,128)S(1)} fusion(f32[5,4,128,128]{2,1,0,3:T(4,128)S(1)} %get-tuple-element.13, f32[5,4,128,128]{2,1,0,3:T(4,128)S(1)} %multiply_dynamic-update-slice_fusion.4, f32[5,4,128,1]{2,1,0,3:T(4,128)S(1)} %get-tuple-element.15, f32[5,4,128,1]{2,1,0,3:T(4,128)S(1)} %fusion.71, ...), kind=kLoop, calls=%fused_computation.137 | loop fusion | flops 6881280 | bytes 4890632 | tf_op jit(solution)/shard_map/stack | solution.py:116
  310.0 5.7 %collective-permute-done.40 = f32[4,5,4,128]{3,2,1,0:T(4,128)S(1)} collective-permute-done((f32[4,5,4,128]{3,2,1,0:T(4,128)S(1)}, f32[4,5,4,128]{3,2,1,0:T(4,128)S(1)}, u32[]{:S(2)}, u32[]{:S(2)}) %collective-permute-start.40) | collective-permute-done | bytes 40992 | tf_op jit(solution)/shard_map/ppermute | solution.py:33
  317.7 5.0 %collective-permute-done.41 = f32[4,5,4,128]{3,2,1,0:T(4,128)S(1)} collective-permute-done((f32[4,5,4,128]{3,2,1,0:T(4,128)S(1)}, f32[4,5,4,128]{3,2,1,0:T(4,128)S(1)}, u32[]{:S(2)}, u32[]{:S(2)}) %collective-permute-start.41) | collective-permute-done | bytes 40992 | tf_op jit(solution)/shard_map/ppermute | solution.py:33
  323.3 5.3 %collective-permute-done.42 = f32[4,5,4,128]{3,2,1,0:T(4,128)S(1)} collective-permute-done((f32[4,5,4,128]{3,2,1,0:T(4,128)S(1)}, f32[4,5,4,128]{3,2,1,0:T(4,128)S(1)}, u32[]{:S(2)}, u32[]{:S(2)}) %collective-permute-start.42) | collective-permute-done | bytes 40992 | tf_op jit(solution)/shard_map/ppermute | solution.py:33
  338.6 5.1 %fusion.41 = (f32[5,4,128,128]{2,1,0,3:T(4,128)S(1)}, f32[5,4,128,128]{2,1,0,3:T(4,128)S(1)}, f32[5,4,128,128]{2,1,0,3:T(4,128)S(1)}) fusion(f32[5,4,128,1]{2,1,0,3:T(4,128)S(1)} %get-tuple-element.10, f32[5,4,128,128]{2,1,0,3:T(4,128)S(1)} %get-tuple-element.8, f32[5,4,128,1]{2,1,0,3:T(4,128)S(1)} %fusion.67, ...), kind=kLoop, calls=%fused_computation.180 | loop fusion | flops 3932160 | bytes 5939200 | tf_op jit(solution)/shard_map/mul | solution.py:47
  354.5 4.9 %subtract_bitcast_fusion = f32[5,1,4,128,128]{3,2,0,4,1:T(4,128)S(1)} fusion(f32[5,4,128,128]{2,1,0,3:T(4,128)S(1)} %get-tuple-element.8, f32[5,4,128,128]{2,1,0,3:T(4,128)S(1)} %multiply_dynamic-update-slice_fusion, f32[5,4,128,1]{2,1,0,3:T(4,128)S(1)} %get-tuple-element.10, f32[5,4,128,1]{2,1,0,3:T(4,128)S(1)} %fusion.67, ...), kind=kLoop, calls=%fused_computation.133 | loop fusion | flops 6881280 | bytes 4890632 | tf_op jit(solution)/shard_map/stack | solution.py:116
  359.4 4.8 %subtract_bitcast_fusion.1 = f32[5,1,4,128,128]{3,2,0,4,1:T(4,128)S(1)} fusion(f32[5,4,128,128]{2,1,0,3:T(4,128)S(1)} %get-tuple-element.7, f32[5,4,128,128]{2,1,0,3:T(4,128)S(1)} %multiply_dynamic-update-slice_fusion.2, f32[5,4,128,1]{2,1,0,3:T(4,128)S(1)} %fusion.69, f32[5,1,128,128]{2,1,0,3:T(1,128)S(1)} %collective-permute-done.44, ...), kind=kLoop, calls=%fused_computation.135 | loop fusion | flops 6553600 | bytes 4880392 | tf_op jit(solution)/shard_map/stack | solution.py:116
  (264 shorter events, 190.5 us)
Async XLA Ops:
  3.3 15.0 %collective-permute-start = (f32[4,5,4,128]{3,2,1,0:T(4,128)S(1)}, f32[4,5,4,128]{3,2,1,0:T(4,128)S(1)}, u32[]{:S(2)}, u32[]{:S(2)}) collective-permute-start(f32[4,5,4,128]{3,2,1,0:T(4,128)S(1)} %pad_maximum_fusion.66), channel_id=1, source_target_pairs={{0,1},{1,2},{2,3},{3,4},{4,5},{5,6},{6,7},{7,8},{8,9},{9,10},{10,1... | collective-permute-start | bytes 122888 | tf_op jit(solution)/shard_map/ppermute | solution.py:33
  6.7 38.2 %collective-permute-start.7 = (f32[5,1,128,128]{2,1,0,3:T(1,128)}, f32[5,1,128,128]{2,1,0,3:T(1,128)S(1)}, u32[]{:S(2)}, u32[]{:S(2)}) collective-permute-start(f32[5,1,128,128]{2,1,0,3:T(1,128)} %get-tuple-element.119), channel_id=1, source_target_pairs={{0,1},{1,2},{2,3},{3,4},{4,5},{5,6},{6,7},{7,8},{8,9},{9,10},{10,1... | collective-permute-start | bytes 983048 | tf_op jit(solution)/shard_map/ppermute | solution.py:21
  9.3 35.6 %collective-permute-start.6 = (f32[5,1,128,128]{2,1,0,3:T(1,128)}, f32[5,1,128,128]{2,1,0,3:T(1,128)}, u32[]{:S(2)}, u32[]{:S(2)}) collective-permute-start(f32[5,1,128,128]{2,1,0,3:T(1,128)} %get-tuple-element.120), channel_id=1, source_target_pairs={{1,0},{2,1},{3,2},{4,3},{5,4},{6,5},{7,6},{8,7},{9,8},{10,9},{11,1... | collective-permute-start | bytes 983048 | tf_op jit(solution)/shard_map/ppermute | solution.py:23
  13.0 44.3 %collective-permute-start.5 = (f32[5,1,128,128]{2,1,0,3:T(1,128)}, f32[5,1,128,128]{2,1,0,3:T(1,128)}, u32[]{:S(2)}, u32[]{:S(2)}) collective-permute-start(f32[5,1,128,128]{2,1,0,3:T(1,128)} %get-tuple-element.114), channel_id=1, source_target_pairs={{0,1},{1,2},{2,3},{3,4},{4,5},{5,6},{6,7},{7,8},{8,9},{9,10},{10,1... | collective-permute-start | bytes 983048 | tf_op jit(solution)/shard_map/ppermute | solution.py:21
  13.0 44.3 %collective-permute-start.4 = (f32[5,1,128,128]{2,1,0,3:T(1,128)}, f32[5,1,128,128]{2,1,0,3:T(1,128)}, u32[]{:S(2)}, u32[]{:S(2)}) collective-permute-start(f32[5,1,128,128]{2,1,0,3:T(1,128)} %get-tuple-element.115), channel_id=1, source_target_pairs={{1,0},{2,1},{3,2},{4,3},{5,4},{6,5},{7,6},{8,7},{9,8},{10,9},{11,1... | collective-permute-start | bytes 983048 | tf_op jit(solution)/shard_map/ppermute | solution.py:23
  31.2 12.8 %collective-permute-start.3 = (f32[4,5,4,128]{3,2,1,0:T(4,128)S(1)}, f32[4,5,4,128]{3,2,1,0:T(4,128)}, u32[]{:S(2)}, u32[]{:S(2)}) collective-permute-start(f32[4,5,4,128]{3,2,1,0:T(4,128)S(1)} %broadcast_select_fusion.17), channel_id=1, source_target_pairs={{0,8},{1,9},{2,10},{3,11},{4,12},{5,13},{6,14},{7,15},{8,0},{9,1},... | collective-permute-start | bytes 122888 | tf_op jit(solution)/shard_map/ppermute | solution.py:33
  99.9 9.5 %collective-permute-start.11 = (f32[4,5,4,128]{3,2,1,0:T(4,128)S(1)}, f32[4,5,4,128]{3,2,1,0:T(4,128)S(1)}, u32[]{:S(2)}, u32[]{:S(2)}) collective-permute-start(f32[4,5,4,128]{3,2,1,0:T(4,128)S(1)} %broadcast_select_fusion.16), channel_id=1, source_target_pairs={{0,8},{1,9},{2,10},{3,11},{4,12},{5,13},{6,14},{7,15},{8,0},{9,1},... | collective-permute-start | bytes 122888 | tf_op jit(solution)/shard_map/ppermute | solution.py:33
  100.4 9.4 %collective-permute-start.15 = (f32[5,1,128,128]{2,1,0,3:T(1,128)S(1)}, f32[5,1,128,128]{2,1,0,3:T(1,128)S(1)}, u32[]{:S(2)}, u32[]{:S(2)}) collective-permute-start(f32[5,1,128,128]{2,1,0,3:T(1,128)S(1)} %get-tuple-element.109), channel_id=1, source_target_pairs={{0,1},{1,2},{2,3},{3,4},{4,5},{5,6},{6,7},{7,8},{8,9},{9,10},{10,1... | collective-permute-start | bytes 983048 | tf_op jit(solution)/shard_map/ppermute | solution.py:21
  100.5 9.3 %collective-permute-start.14 = (f32[5,1,128,128]{2,1,0,3:T(1,128)S(1)}, f32[5,1,128,128]{2,1,0,3:T(1,128)S(1)}, u32[]{:S(2)}, u32[]{:S(2)}) collective-permute-start(f32[5,1,128,128]{2,1,0,3:T(1,128)S(1)} %get-tuple-element.110), channel_id=1, source_target_pairs={{1,0},{2,1},{3,2},{4,3},{5,4},{6,5},{7,6},{8,7},{9,8},{10,9},{11,1... | collective-permute-start | bytes 983048 | tf_op jit(solution)/shard_map/ppermute | solution.py:23
  104.9 13.0 %collective-permute-start.13 = (f32[5,1,128,128]{2,1,0,3:T(1,128)S(1)}, f32[5,1,128,128]{2,1,0,3:T(1,128)S(1)}, u32[]{:S(2)}, u32[]{:S(2)}) collective-permute-start(f32[5,1,128,128]{2,1,0,3:T(1,128)S(1)} %get-tuple-element.104), channel_id=1, source_target_pairs={{0,1},{1,2},{2,3},{3,4},{4,5},{5,6},{6,7},{7,8},{8,9},{9,10},{10,1... | collective-permute-start | bytes 983048 | tf_op jit(solution)/shard_map/ppermute | solution.py:21
  104.9 13.0 %collective-permute-start.12 = (f32[5,1,128,128]{2,1,0,3:T(1,128)S(1)}, f32[5,1,128,128]{2,1,0,3:T(1,128)S(1)}, u32[]{:S(2)}, u32[]{:S(2)}) collective-permute-start(f32[5,1,128,128]{2,1,0,3:T(1,128)S(1)} %get-tuple-element.105), channel_id=1, source_target_pairs={{1,0},{2,1},{3,2},{4,3},{5,4},{6,5},{7,6},{8,7},{9,8},{10,9},{11,1... | collective-permute-start | bytes 983048 | tf_op jit(solution)/shard_map/ppermute | solution.py:23
  157.3 9.5 %collective-permute-start.19 = (f32[4,5,4,128]{3,2,1,0:T(4,128)S(1)}, f32[4,5,4,128]{3,2,1,0:T(4,128)S(1)}, u32[]{:S(2)}, u32[]{:S(2)}) collective-permute-start(f32[4,5,4,128]{3,2,1,0:T(4,128)S(1)} %broadcast_select_fusion.15), channel_id=1, source_target_pairs={{0,8},{1,9},{2,10},{3,11},{4,12},{5,13},{6,14},{7,15},{8,0},{9,1},... | collective-permute-start | bytes 122888 | tf_op jit(solution)/shard_map/ppermute | solution.py:33
  157.8 9.4 %collective-permute-start.23 = (f32[5,1,128,128]{2,1,0,3:T(1,128)S(1)}, f32[5,1,128,128]{2,1,0,3:T(1,128)S(1)}, u32[]{:S(2)}, u32[]{:S(2)}) collective-permute-start(f32[5,1,128,128]{2,1,0,3:T(1,128)S(1)} %get-tuple-element.99), channel_id=1, source_target_pairs={{0,1},{1,2},{2,3},{3,4},{4,5},{5,6},{6,7},{7,8},{8,9},{9,10},{10,1... | collective-permute-start | bytes 983048 | tf_op jit(solution)/shard_map/ppermute | solution.py:21
  157.9 9.3 %collective-permute-start.22 = (f32[5,1,128,128]{2,1,0,3:T(1,128)S(1)}, f32[5,1,128,128]{2,1,0,3:T(1,128)S(1)}, u32[]{:S(2)}, u32[]{:S(2)}) collective-permute-start(f32[5,1,128,128]{2,1,0,3:T(1,128)S(1)} %get-tuple-element.100), channel_id=1, source_target_pairs={{1,0},{2,1},{3,2},{4,3},{5,4},{6,5},{7,6},{8,7},{9,8},{10,9},{11,1... | collective-permute-start | bytes 983048 | tf_op jit(solution)/shard_map/ppermute | solution.py:23
  162.3 13.0 %collective-permute-start.21 = (f32[5,1,128,128]{2,1,0,3:T(1,128)S(1)}, f32[5,1,128,128]{2,1,0,3:T(1,128)S(1)}, u32[]{:S(2)}, u32[]{:S(2)}) collective-permute-start(f32[5,1,128,128]{2,1,0,3:T(1,128)S(1)} %get-tuple-element.94), channel_id=1, source_target_pairs={{0,1},{1,2},{2,3},{3,4},{4,5},{5,6},{6,7},{7,8},{8,9},{9,10},{10,1... | collective-permute-start | bytes 983048 | tf_op jit(solution)/shard_map/ppermute | solution.py:21
  162.3 13.1 %collective-permute-start.20 = (f32[5,1,128,128]{2,1,0,3:T(1,128)S(1)}, f32[5,1,128,128]{2,1,0,3:T(1,128)S(1)}, u32[]{:S(2)}, u32[]{:S(2)}) collective-permute-start(f32[5,1,128,128]{2,1,0,3:T(1,128)S(1)} %get-tuple-element.95), channel_id=1, source_target_pairs={{1,0},{2,1},{3,2},{4,3},{5,4},{6,5},{7,6},{8,7},{9,8},{10,9},{11,1... | collective-permute-start | bytes 983048 | tf_op jit(solution)/shard_map/ppermute | solution.py:23
  201.2 7.1 %collective-permute-start.25 = (f32[4,5,4,128]{3,2,1,0:T(4,128)S(1)}, f32[4,5,4,128]{3,2,1,0:T(4,128)S(1)}, u32[]{:S(2)}, u32[]{:S(2)}) collective-permute-start(f32[4,5,4,128]{3,2,1,0:T(4,128)S(1)} %broadcast_select_fusion.2), channel_id=1, source_target_pairs={{0,2},{1,3},{2,4},{3,5},{4,6},{5,7},{6,8},{7,9},{8,10},{9,11},{10,... | collective-permute-start | bytes 122888 | tf_op jit(solution)/shard_map/ppermute | solution.py:33
  214.3 9.5 %collective-permute-start.27 = (f32[4,5,4,128]{3,2,1,0:T(4,128)S(1)}, f32[4,5,4,128]{3,2,1,0:T(4,128)S(1)}, u32[]{:S(2)}, u32[]{:S(2)}) collective-permute-start(f32[4,5,4,128]{3,2,1,0:T(4,128)S(1)} %broadcast_select_fusion.14), channel_id=1, source_target_pairs={{0,8},{1,9},{2,10},{3,11},{4,12},{5,13},{6,14},{7,15},{8,0},{9,1},... | collective-permute-start | bytes 122888 | tf_op jit(solution)/shard_map/ppermute | solution.py:33
  214.9 9.4 %collective-permute-start.31 = (f32[5,1,128,128]{2,1,0,3:T(1,128)S(1)}, f32[5,1,128,128]{2,1,0,3:T(1,128)S(1)}, u32[]{:S(2)}, u32[]{:S(2)}) collective-permute-start(f32[5,1,128,128]{2,1,0,3:T(1,128)S(1)} %get-tuple-element.89), channel_id=1, source_target_pairs={{0,1},{1,2},{2,3},{3,4},{4,5},{5,6},{6,7},{7,8},{8,9},{9,10},{10,1... | collective-permute-start | bytes 983048 | tf_op jit(solution)/shard_map/ppermute | solution.py:21
  214.9 9.3 %collective-permute-start.30 = (f32[5,1,128,128]{2,1,0,3:T(1,128)S(1)}, f32[5,1,128,128]{2,1,0,3:T(1,128)S(1)}, u32[]{:S(2)}, u32[]{:S(2)}) collective-permute-start(f32[5,1,128,128]{2,1,0,3:T(1,128)S(1)} %get-tuple-element.90), channel_id=1, source_target_pairs={{1,0},{2,1},{3,2},{4,3},{5,4},{6,5},{7,6},{8,7},{9,8},{10,9},{11,1... | collective-permute-start | bytes 983048 | tf_op jit(solution)/shard_map/ppermute | solution.py:23
  219.4 13.0 %collective-permute-start.29 = (f32[5,1,128,128]{2,1,0,3:T(1,128)S(1)}, f32[5,1,128,128]{2,1,0,3:T(1,128)S(1)}, u32[]{:S(2)}, u32[]{:S(2)}) collective-permute-start(f32[5,1,128,128]{2,1,0,3:T(1,128)S(1)} %get-tuple-element.84), channel_id=1, source_target_pairs={{0,1},{1,2},{2,3},{3,4},{4,5},{5,6},{6,7},{7,8},{8,9},{9,10},{10,1... | collective-permute-start | bytes 983048 | tf_op jit(solution)/shard_map/ppermute | solution.py:21
  219.4 13.1 %collective-permute-start.28 = (f32[5,1,128,128]{2,1,0,3:T(1,128)S(1)}, f32[5,1,128,128]{2,1,0,3:T(1,128)S(1)}, u32[]{:S(2)}, u32[]{:S(2)}) collective-permute-start(f32[5,1,128,128]{2,1,0,3:T(1,128)S(1)} %get-tuple-element.85), channel_id=1, source_target_pairs={{1,0},{2,1},{3,2},{4,3},{5,4},{6,5},{7,6},{8,7},{9,8},{10,9},{11,1... | collective-permute-start | bytes 983048 | tf_op jit(solution)/shard_map/ppermute | solution.py:23
  271.1 9.5 %collective-permute-start.35 = (f32[4,5,4,128]{3,2,1,0:T(4,128)S(1)}, f32[4,5,4,128]{3,2,1,0:T(4,128)S(1)}, u32[]{:S(2)}, u32[]{:S(2)}) collective-permute-start(f32[4,5,4,128]{3,2,1,0:T(4,128)S(1)} %broadcast_select_fusion.13), channel_id=1, source_target_pairs={{0,8},{1,9},{2,10},{3,11},{4,12},{5,13},{6,14},{7,15},{8,0},{9,1},... | collective-permute-start | bytes 122888 | tf_op jit(solution)/shard_map/ppermute | solution.py:33
  271.7 9.4 %collective-permute-start.39 = (f32[5,1,128,128]{2,1,0,3:T(1,128)S(1)}, f32[5,1,128,128]{2,1,0,3:T(1,128)S(1)}, u32[]{:S(2)}, u32[]{:S(2)}) collective-permute-start(f32[5,1,128,128]{2,1,0,3:T(1,128)S(1)} %get-tuple-element.79), channel_id=1, source_target_pairs={{0,1},{1,2},{2,3},{3,4},{4,5},{5,6},{6,7},{7,8},{8,9},{9,10},{10,1... | collective-permute-start | bytes 983048 | tf_op jit(solution)/shard_map/ppermute | solution.py:21
  271.8 9.3 %collective-permute-start.38 = (f32[5,1,128,128]{2,1,0,3:T(1,128)S(1)}, f32[5,1,128,128]{2,1,0,3:T(1,128)S(1)}, u32[]{:S(2)}, u32[]{:S(2)}) collective-permute-start(f32[5,1,128,128]{2,1,0,3:T(1,128)S(1)} %get-tuple-element.80), channel_id=1, source_target_pairs={{1,0},{2,1},{3,2},{4,3},{5,4},{6,5},{7,6},{8,7},{9,8},{10,9},{11,1... | collective-permute-start | bytes 983048 | tf_op jit(solution)/shard_map/ppermute | solution.py:23
  276.2 13.0 %collective-permute-start.37 = (f32[5,1,128,128]{2,1,0,3:T(1,128)S(1)}, f32[5,1,128,128]{2,1,0,3:T(1,128)S(1)}, u32[]{:S(2)}, u32[]{:S(2)}) collective-permute-start(f32[5,1,128,128]{2,1,0,3:T(1,128)S(1)} %get-tuple-element.74), channel_id=1, source_target_pairs={{0,1},{1,2},{2,3},{3,4},{4,5},{5,6},{6,7},{7,8},{8,9},{9,10},{10,1... | collective-permute-start | bytes 983048 | tf_op jit(solution)/shard_map/ppermute | solution.py:21
  276.2 13.0 %collective-permute-start.36 = (f32[5,1,128,128]{2,1,0,3:T(1,128)S(1)}, f32[5,1,128,128]{2,1,0,3:T(1,128)S(1)}, u32[]{:S(2)}, u32[]{:S(2)}) collective-permute-start(f32[5,1,128,128]{2,1,0,3:T(1,128)S(1)} %get-tuple-element.75), channel_id=1, source_target_pairs={{1,0},{2,1},{3,2},{4,3},{5,4},{6,5},{7,6},{8,7},{9,8},{10,9},{11,1... | collective-permute-start | bytes 983048 | tf_op jit(solution)/shard_map/ppermute | solution.py:23
  328.7 9.5 %collective-permute-start.43 = (f32[4,5,4,128]{3,2,1,0:T(4,128)S(1)}, f32[4,5,4,128]{3,2,1,0:T(4,128)S(1)}, u32[]{:S(2)}, u32[]{:S(2)}) collective-permute-start(f32[4,5,4,128]{3,2,1,0:T(4,128)S(1)} %broadcast_select_fusion.12), channel_id=1, source_target_pairs={{0,8},{1,9},{2,10},{3,11},{4,12},{5,13},{6,14},{7,15},{8,0},{9,1},... | collective-permute-start | bytes 122888 | tf_op jit(solution)/shard_map/ppermute | solution.py:33
  329.2 9.4 %collective-permute-start.47 = (f32[5,1,128,128]{2,1,0,3:T(1,128)S(1)}, f32[5,1,128,128]{2,1,0,3:T(1,128)S(1)}, u32[]{:S(2)}, u32[]{:S(2)}) collective-permute-start(f32[5,1,128,128]{2,1,0,3:T(1,128)S(1)} %get-tuple-element.69), channel_id=1, source_target_pairs={{0,1},{1,2},{2,3},{3,4},{4,5},{5,6},{6,7},{7,8},{8,9},{9,10},{10,1... | collective-permute-start | bytes 983048 | tf_op jit(solution)/shard_map/ppermute | solution.py:21
  329.3 9.3 %collective-permute-start.46 = (f32[5,1,128,128]{2,1,0,3:T(1,128)S(1)}, f32[5,1,128,128]{2,1,0,3:T(1,128)S(1)}, u32[]{:S(2)}, u32[]{:S(2)}) collective-permute-start(f32[5,1,128,128]{2,1,0,3:T(1,128)S(1)} %get-tuple-element.70), channel_id=1, source_target_pairs={{1,0},{2,1},{3,2},{4,3},{5,4},{6,5},{7,6},{8,7},{9,8},{10,9},{11,1... | collective-permute-start | bytes 983048 | tf_op jit(solution)/shard_map/ppermute | solution.py:23
  333.7 13.0 %collective-permute-start.45 = (f32[5,1,128,128]{2,1,0,3:T(1,128)S(1)}, f32[5,1,128,128]{2,1,0,3:T(1,128)S(1)}, u32[]{:S(2)}, u32[]{:S(2)}) collective-permute-start(f32[5,1,128,128]{2,1,0,3:T(1,128)S(1)} %get-tuple-element.64), channel_id=1, source_target_pairs={{0,1},{1,2},{2,3},{3,4},{4,5},{5,6},{6,7},{7,8},{8,9},{9,10},{10,1... | collective-permute-start | bytes 983048 | tf_op jit(solution)/shard_map/ppermute | solution.py:21
  333.7 13.1 %collective-permute-start.44 = (f32[5,1,128,128]{2,1,0,3:T(1,128)S(1)}, f32[5,1,128,128]{2,1,0,3:T(1,128)S(1)}, u32[]{:S(2)}, u32[]{:S(2)}) collective-permute-start(f32[5,1,128,128]{2,1,0,3:T(1,128)S(1)} %get-tuple-element.65), channel_id=1, source_target_pairs={{1,0},{2,1},{3,2},{4,3},{5,4},{6,5},{7,6},{8,7},{9,8},{10,9},{11,1... | collective-permute-start | bytes 983048 | tf_op jit(solution)/shard_map/ppermute | solution.py:23
  (28 other events, 166.8 us)
where the time goes:
time: 379 us; the launch traced here: 372 us
  other arithmetic  193 us (51%)
  waiting for transfers between devices  86.4 us (23%)
  starting transfers between devices  56.7 us (15%)
  local copies, waits for them, and re-layouts  26.6 us (7%)
  between operations  8.99 us (2%)
    ppermute x24, waiting for transfers between devices, from_behind(): return lax.ppermute(value, axis, pairs)  85 us
    mul x12, other arithmetic, operator_terms(): axial_diff = (axial_pad[..., 2:] - axial_pad[..., :-2]) * 0.5  62.9 us
    another operation x12, other arithmetic, per_device(): terms = jnp.stack([rotor_terms, stator_terms], axis=1)  60.2 us
    ppermute x12, starting transfers between devices, with_halo(): lax.ppermute(head, axis, [((i + 1) % count, i) for i in range(count)])  51.2 us
    unnamed x48, other arithmetic  36.1 us
    mul x6, other arithmetic, operator_terms(): center[:, :, :1] * wall_sign  14.8 us
    sub x6, other arithmetic, per_device(): start_field - weight * PSEUDO_STEP * (terms + 1.5 / PHYS_STEP * field + f...  14.6 us
    unnamed x26, local copies, waits for them, and re-layouts  9.13 us
  transfers between devices with their start and end apart: 48, of which 22 were waited for; matrix products, arithmetic and copies ran while one was open for 23% of the time, Pallas kernels for 0%

commit v1 on v0

v1 whole, which is shorter than its diff:
```python
import functools
import jax
import jax.numpy as jnp
from jax import lax
from jax.experimental import pallas as pl
from jax.experimental.pallas import tpu as pltpu
from jax.sharding import PartitionSpec as P

ITERS = 2
PSEUDO_STEP = 0.2
PHYS_STEP = 1.0
SECTIONS = 3
WEIGHT_EARLY = 0.6
WEIGHT_LAST = 1.0
PAD = 8
CHUNK = 32


def exchange_levels(count):
    levels = []
    stride = 1
    while stride < count:
        radix = 4 if (count // stride) % 4 == 0 else count // stride
        levels.append((stride, radix))
        stride *= radix
    return levels[::-1]


def exchange_messages(count):
    out = []
    for level, (stride, radix) in enumerate(exchange_levels(count)):
        top = radix if stride > 1 else radix + 1
        for j in range(1, top):
            for row in range(2):
                out.append((level, stride * j, row))
    return out


def kernel(
    count, cells, radial,
    scal_ref, digit_ref, now_ref, prev_ref, eddy_ref,
    out_ref,
    fbuf, base, fixed, gcol, ifs, ifr, load_sem, hsend, hrecv, isend, irecv,
):
    me = lax.axis_index("theta")
    levels = exchange_levels(count)
    messages = exchange_messages(count)
    total = ITERS * SECTIONS
    width = fbuf.shape[-1]
    block = ifs.shape[-2]

    def peer(steps):
        return {"theta": lax.rem(me + (steps % count), count)}

    loads = [
        pltpu.make_async_copy(
            now_ref, fbuf.at[0, :, :, pl.ds(1, cells), pl.ds(PAD, radial)], load_sem.at[0]
        ),
        pltpu.make_async_copy(now_ref, base, load_sem.at[1]),
        pltpu.make_async_copy(prev_ref, fixed, load_sem.at[2]),
    ]
    for load in loads:
        load.start()

    reach = {1 % count, count - 1}
    for _, steps, _ in messages:
        reach |= {steps % count, -steps % count}
    reach = sorted(reach - {0})
    barrier = pltpu.get_barrier_semaphore()
    for steps in reach:
        pl.semaphore_signal(
            barrier, inc=1, device_id=peer(steps), device_id_type=pl.DeviceIdType.MESH
        )
    pl.semaphore_wait(barrier, len(reach))

    def halo(slot, row, side):
        source, target = (1, cells + 1) if side == 0 else (cells, 0)
        return pltpu.make_async_remote_copy(
            src_ref=fbuf.at[slot, :, row, source, pl.ds(PAD, radial)],
            dst_ref=fbuf.at[slot, :, row, target, pl.ds(PAD, radial)],
            send_sem=hsend.at[slot, row, side],
            recv_sem=hrecv.at[slot, row, side],
            device_id=peer(-1 if side == 0 else 1),
            device_id_type=pl.DeviceIdType.MESH,
        )

    def plane_message(slot, index):
        level, steps, row = messages[index]
        return pltpu.make_async_remote_copy(
            src_ref=ifs.at[slot, level, row],
            dst_ref=ifr.at[slot, index],
            send_sem=isend.at[slot, index],
            recv_sem=irecv.at[slot, index],
            device_id=peer(steps if row == 0 else -steps),
            device_id_type=pl.DeviceIdType.MESH,
        )

    def of_level(level):
        return [index for index, message in enumerate(messages) if message[0] == level]

    def ghosts(slot, row, t):
        for c in range(5):
            sign = -1.0 if c == 3 else 1.0
            fbuf[slot, c, row, t, pl.ds(PAD - 1, 1), :] = (
                sign * fbuf[slot, c, row, t, pl.ds(PAD, 1), :]
            )
            fbuf[slot, c, row, t, pl.ds(PAD + radial, 1), :] = (
                sign * fbuf[slot, c, row, t, pl.ds(PAD + radial - 1, 1), :]
            )

    lane = lax.broadcasted_iota(jnp.int32, (radial, width), 1)

    def pack(slot):
        acc = jnp.zeros((radial, width), jnp.float32)
        for row in range(2):
            edge = width - 1 if row == 0 else 0
            for t in range(cells):
                for c in range(5):
                    j = row * block + t * 5 + c
                    plane = fbuf[slot, c, row, t + 1, pl.ds(PAD, radial), :]
                    acc = jnp.where(lane == j, pltpu.roll(plane, (j - edge) % width, 1), acc)
        turned = acc.T
        for row in range(2):
            ifs[slot, 0, row] = turned[row * block : (row + 1) * block]

    def publish(slot):
        pack(slot)
        for index in of_level(0):
            plane_message(slot, index).start()
        for row in range(2):
            for side in range(2):
                halo(slot, row, side).start()

    def pick(values, digit):
        out = values[0]
        for j in range(1, len(values)):
            out = jnp.where(digit == j, values[j], out)
        return out

    def interface(slot):
        near = far = None
        for level, (stride, radix) in enumerate(levels):
            got = ([ifs[slot, level, 0]], [ifs[slot, level, 1]])
            for index in of_level(level):
                plane_message(slot, index).wait()
            for index in of_level(level):
                got[messages[index][2]].append(ifr[slot, index])
            digit = digit_ref[level]
            near = [pick(got[row][:radix], digit) for row in range(2)]
            if stride > 1:
                for row in range(2):
                    ifs[slot, level + 1, row] = near[row]
                for index in of_level(level + 1):
                    plane_message(slot, index).start()
            else:
                far = [pick(got[row][1 : radix + 1], digit) for row in range(2)]
        used = 5 * cells
        within = digit_ref[len(levels)]
        from_rotor = jnp.concatenate([far[0][:used], near[0][:used]], axis=0)
        from_stator = jnp.concatenate([near[1][:used], far[1][:used]], axis=0)
        low = pick(
            [from_rotor[5 * (cells - m) : 5 * (2 * cells - m)] for m in range(cells)], within
        )
        high = pick([from_stator[5 * m : 5 * (m + cells)] for m in range(cells)], within)
        gap = jnp.zeros((block - used, width), jnp.float32)
        rest = jnp.zeros((width - 2 * block, width), jnp.float32)
        gcol[...] = jnp.concatenate([high, gap, low, gap, rest], axis=0).T

    small = lax.broadcasted_iota(jnp.int32, (CHUNK, width), 1)
    is_first = small == 0
    is_last = small == width - 1

    def layer(slot, new, row, t, k):
        half_u = scal_ref[row, 0] * (0.5 * k)
        half_v = scal_ref[row, 1] * (0.5 * k)
        push_rho = scal_ref[row, 2] * (0.5 * k)
        push_inv = scal_ref[row, 3] * (0.5 * k)
        push_p = scal_ref[row, 4] * (0.5 * k)

        def body(i, carry):
            r0 = pl.multiple_of(i * CHUNK, CHUNK)
            ke = eddy_ref[row, t - 1, pl.ds(r0, CHUNK), :] * k
            cf = ke * 6.0 + (1.5 / PHYS_STEP) * k
            columns = gcol[pl.ds(r0, CHUNK), :]
            partial = []
            extra = {}
            div = None
            for c in range(5):
                f = fbuf[slot, c, row, t, pl.ds(r0 + PAD, CHUNK), :]
                rm = fbuf[slot, c, row, t, pl.ds(r0 + (PAD - 1), CHUNK), :]
                rp = fbuf[slot, c, row, t, pl.ds(r0 + (PAD + 1), CHUNK), :]
                tm = fbuf[slot, c, row, t - 1, pl.ds(r0 + PAD, CHUNK), :]
                tp = fbuf[slot, c, row, t + 1, pl.ds(r0 + PAD, CHUNK), :]
                am = pltpu.roll(f, 1, 1)
                ap = pltpu.roll(f, width - 1, 1)
                j = row * block + (t - 1) * 5 + c
                if row == 0:
                    am = jnp.where(is_first, 0.0, am)
                    ap = jnp.where(is_last, pltpu.roll(columns, width - 1 - j, 1), ap)
                else:
                    am = jnp.where(
                        is_first, pltpu.roll(columns, (width - j) % width, 1), am
                    )
                    ap = jnp.where(is_last, f, ap)
                da = ap - am
                dt = tp - tm
                around = (ap + am) + (tp + tm) + (rp + rm)
                value = (
                    base[c, row, t - 1, pl.ds(r0, CHUNK), :]
                    - k * fixed[c, row, t - 1, pl.ds(r0, CHUNK), :]
                    - cf * f
                    + ke * around
                    - half_u * da
                    - half_v * dt
                )
                if c == 1:
                    div = da
                elif c == 2:
                    div = div + dt
                elif c == 3:
                    div = div + (rp - rm)
                elif c == 4:
                    extra = {1: da, 2: dt, 3: rp - rm}
                partial.append(value)
            for c in range(5):
                if c == 0:
                    value = partial[0] - push_rho * div
                elif c == 4:
                    value = partial[4] - push_p * div
                else:
                    value = partial[c] - push_inv * extra[c]
                fbuf[new, c, row, t, pl.ds(r0 + PAD, CHUNK), :] = value
            return carry

        lax.fori_loop(0, radial // CHUNK, body, 0)
        ghosts(new, row, t)

    for load in loads:
        load.wait()
    for row in range(2):
        for t in range(cells):
            ghosts(0, row, t + 1)
    publish(0)

    def prepare(t, carry):
        for c in range(5):
            for row in range(2):
                fixed[c, row, t] = (0.5 / PHYS_STEP) * fixed[c, row, t] - (
                    2.0 / PHYS_STEP
                ) * base[c, row, t]
        return carry

    lax.fori_loop(0, cells, prepare, 0)

    def section(s, carry):
        slot = lax.rem(s, 2)
        new = 1 - slot
        k = jnp.where(
            lax.rem(s, SECTIONS) == SECTIONS - 1,
            jnp.float32(WEIGHT_LAST * PSEUDO_STEP),
            jnp.float32(WEIGHT_EARLY * PSEUDO_STEP),
        )

        @pl.when(jnp.logical_and(s > 0, lax.rem(s, SECTIONS) == 0))
        def _():
            def keep(t, carry):
                for c in range(5):
                    for row in range(2):
                        base[c, row, t] = fbuf[slot, c, row, t + 1, pl.ds(PAD, radial), :]
                return carry

            lax.fori_loop(0, cells, keep, 0)

        interface(slot)
        for row in range(2):
            for t in range(2, cells):
                layer(slot, new, row, t, k)

        @pl.when(s > 0)
        def _():
            for row in range(2):
                for side in range(2):
                    halo(new, row, side).wait_send()

        for row in range(2):
            halo(slot, row, 1).wait_recv()
            if cells == 1:
                halo(slot, row, 0).wait_recv()
            layer(slot, new, row, 1, k)
            if cells > 1:
                halo(slot, row, 0).wait_recv()
                layer(slot, new, row, cells, k)

        @pl.when(s < total - 1)
        def _():
            publish(new)

        return carry

    lax.fori_loop(0, total, section, 0)
    for row in range(2):
        for side in range(2):
            halo((total - 1) % 2, row, side).wait_send()
    store = pltpu.make_async_copy(
        fbuf.at[total % 2, :, :, pl.ds(1, cells), pl.ds(PAD, radial)], out_ref, load_sem.at[0]
    )
    store.start()
    store.wait()


def per_device(state_now, state_prev, eddy_visc, mean_flow, offset):
    _, _, cells, radial, width = state_now.shape
    count = lax.axis_size("theta")
    levels = exchange_levels(count)
    messages = exchange_messages(count)
    shift_cells = offset[0] % (cells * count)
    sectors = shift_cells // cells
    digits = jnp.stack(
        [sectors // stride % radix for stride, radix in levels] + [shift_cells % cells]
    ).astype(jnp.int32)
    scalars = jnp.stack(
        [
            mean_flow[:, 0],
            mean_flow[:, 1],
            mean_flow[:, 2],
            1.0 / mean_flow[:, 2],
            mean_flow[:, 2] * mean_flow[:, 3] * mean_flow[:, 3],
        ],
        axis=1,
    )
    block = -(-5 * cells // 8) * 8
    f32 = jnp.float32
    return pl.pallas_call(
        functools.partial(kernel, count, cells, radial),
        out_shape=jax.ShapeDtypeStruct(state_now.shape, f32),
        in_specs=[
            pl.BlockSpec(memory_space=pltpu.SMEM),
            pl.BlockSpec(memory_space=pltpu.SMEM),
            pl.BlockSpec(memory_space=pl.ANY),
            pl.BlockSpec(memory_space=pl.ANY),
            pl.BlockSpec(memory_space=pltpu.VMEM),
        ],
        out_specs=pl.BlockSpec(memory_space=pl.ANY),
        scratch_shapes=[
            pltpu.VMEM((2, 5, 2, cells + 2, radial + 2 * PAD, width), f32),
            pltpu.VMEM((5, 2, cells, radial, width), f32),
            pltpu.VMEM((5, 2, cells, radial, width), f32),
            pltpu.VMEM((radial, width), f32),
            pltpu.VMEM((2, len(levels), 2, block, radial), f32),
            pltpu.VMEM((2, len(messages), block, radial), f32),
            pltpu.SemaphoreType.DMA((3,)),
            pltpu.SemaphoreType.DMA((2, 2, 2)),
            pltpu.SemaphoreType.DMA((2, 2, 2)),
            pltpu.SemaphoreType.DMA((2, len(messages))),
            pltpu.SemaphoreType.DMA((2, len(messages))),
        ],
        compiler_params=pltpu.CompilerParams(
            collective_id=0, has_side_effects=True, vmem_limit_bytes=48 * 1024 * 1024
        ),
    )(scalars, digits, state_now, state_prev, eddy_visc)


def solution(mesh):
    placed = (
        P(None, None, "theta", "groups", None),
        P(None, None, "theta", "groups", None),
        P(None, "theta", "groups", None),
        P(),
        P("groups"),
    )
    return jax.shard_map(
        per_device,
        mesh=mesh,
        in_specs=placed,
        out_specs=P(None, None, "theta", "groups", None),
        check_vma=False,
    )
```

time: 379 us -> 152 us (0.40); the launches traced: 372 us -> 152 us
  other arithmetic: 193 us -> 1.66 us
  Pallas kernels: 0 us -> 145 us
  waiting for transfers between devices: 86.4 us -> 0 us
  starting transfers between devices: 56.7 us -> 0 us
  local copies, waits for them, and re-layouts: 26.6 us -> 4.28 us
  between operations: 8.99 us -> 0.75 us
    pallas_call x0 -> x1, Pallas kernels: none -> 145 us  [per_device(): pl.pallas_call(functools.partial(kernel, count, cells, radial), out_shape...]
    ppermute x48 -> x0, waiting for transfers between devices: 86.4 us -> none  [the longest x24 85 us: from_behind(): return lax.ppermute(value, axis, pairs)]
    mul x18 -> x0, other arithmetic: 77.7 us -> none  [the longest x12 62.9 us: operator_terms(): axial_diff = (axial_pad[..., 2:] - axial_pad[..., :-2]) * 0.5]
    another operation x30 -> x2, other arithmetic: 61.9 us -> 0.83 us  [the longest x1 0.75 us: per_device(): jnp.stack([mean_flow[:, 0], mean_flow[:, 1], mean_flow[:, 2], 1.0 / mean_...]
    ppermute x48 -> x0, starting transfers between devices: 56.7 us -> none  [the longest x12 51.2 us: with_halo(): lax.ppermute(head, axis, [((i + 1) % count, i) for i in range(count)])]
    unnamed x48 -> x0, other arithmetic: 36.1 us -> none
    sub x6 -> x0, other arithmetic: 14.6 us -> none  [per_device(): start_field - weight * PSEUDO_STEP * (terms + 1.5 / PHYS_STEP * field + f...]
    slice x13 -> x0, local copies, waits for them, and re-layouts: 8.47 us -> none  [the longest x12 7.78 us: with_halo(): lax.slice_in_dim(cells, cells.shape[dim] - width, cells.shape[dim], axis=...]
  transfers between devices with their start and end apart: 48 -> 0, of which waited for: 22 -> 0; matrix products, arithmetic and copies ran while one was open for 23% -> 0% of each run, Pallas kernels for 0% -> 0%
where the time goes in v1:
time: 152 us
  Pallas kernels  145 us (95%)
  local copies, waits for them, and re-layouts  4.28 us (3%)
  other arithmetic  1.66 us (1%)
    pallas_call x1, Pallas kernels, per_device(): pl.pallas_call(functools.partial(kernel, count, cells, radial), out_shape...  145 us
    unnamed x5, local copies, waits for them, and re-layouts  4.28 us

profile of v1, /device:TPU:0, one launch (start us, length us, event | category | flops | bytes accessed | tf_op | source)
XLA Modules:
  0.0 151.7 jit_solution(5544260722312067165)
XLA Ops:
  0.7 0.1 pad_add_fusion.digit_ref
  0.8 0.8 slice_divide_fusion
  1.6 0.8 pad_maximum_fusion.scal_ref
  2.4 0.0 copy-start
  2.4 1.7 %copy-done = f32[5,2,4,128,128]{4,3,2,1,0:T(8,128)S(1)} copy-done((f32[5,2,4,128,128]{4,3,2,1,0:T(8,128)S(1)}, f32[5,2,4,128,128]{4,3,2,1,0:T(8,128)}, u32[]{:S(2)}) %copy-start) | copy-done | bytes 2621464
  4.1 0.0 copy-start.1
  4.1 1.0 copy-done.1
  5.2 145.0 %shard_map.55 = f32[5,2,4,128,128]{4,3,2,1,0:T(8,128)S(1)} custom-call(f32[2,5]{1,0:T(2,128)S(1)} %pad_maximum_fusion.scal_ref, s32[3]{0:T(128)S(1)} %pad_add_fusion.digit_ref, f32[5,2,4,128,128]{4,3,2,1,0:T(8,128)S(1)} %copy-done, f32[5,2,4,128,128]{4,3,2,1,0:T(8,128)} %prev_ref.1, f32[2,4,128,128]{3,2,1,0:T(8,128)S(1)} %copy-done.1), custom_call_target="tpu_custom_call" | custom-call | tf_op jit(solution)/shard_map/pallas_call | solution.py:333
  150.2 1.5 copy.8
Async XLA Ops:
  2.4 1.7 %copy-start = (f32[5,2,4,128,128]{4,3,2,1,0:T(8,128)S(1)}, f32[5,2,4,128,128]{4,3,2,1,0:T(8,128)}, u32[]{:S(2)}) copy-start(f32[5,2,4,128,128]{4,3,2,1,0:T(8,128)} %now_ref.1) | copy-start | bytes 7864324
  4.1 1.0 copy-start.1

commit v2 on v1

--- a/solution.py
+++ b/solution.py
@@ -13,7 +13,7 @@
 WEIGHT_EARLY = 0.6
 WEIGHT_LAST = 1.0
 PAD = 8
-CHUNK = 32
+CHUNK = 64
 
 
 def exchange_levels(count):
@@ -40,7 +40,7 @@
     count, cells, radial,
     scal_ref, digit_ref, now_ref, prev_ref, eddy_ref,
     out_ref,
-    fbuf, base, fixed, gcol, ifs, ifr, load_sem, hsend, hrecv, isend, irecv,
+    fbuf, base, fixed, gcol, packed, ifs, ifr, load_sem, hsend, hrecv, isend, irecv,
 ):
     me = lax.axis_index("theta")
     levels = exchange_levels(count)
@@ -110,26 +110,25 @@
 
     lane = lax.broadcasted_iota(jnp.int32, (radial, width), 1)
 
-    def pack(slot):
-        acc = jnp.zeros((radial, width), jnp.float32)
-        for row in range(2):
-            edge = width - 1 if row == 0 else 0
-            for t in range(cells):
-                for c in range(5):
-                    j = row * block + t * 5 + c
-                    plane = fbuf[slot, c, row, t + 1, pl.ds(PAD, radial), :]
-                    acc = jnp.where(lane == j, pltpu.roll(plane, (j - edge) % width, 1), acc)
-        turned = acc.T
-        for row in range(2):
-            ifs[slot, 0, row] = turned[row * block : (row + 1) * block]
-
-    def publish(slot):
-        pack(slot)
+    def pack(slot, row, layers, fresh):
+        acc = jnp.zeros((radial, width), jnp.float32) if fresh else packed[row]
+        edge = width - 1 if row == 0 else 0
+        for t in layers:
+            for c in range(5):
+                j = (t - 1) * 5 + c
+                plane = fbuf[slot, c, row, t, pl.ds(PAD, radial), :]
+                acc = jnp.where(lane == j, pltpu.roll(plane, (j - edge) % width, 1), acc)
+        packed[row] = acc
+
+    def send_plane(slot, row):
+        ifs[slot, 0, row] = packed[row].T[:block]
         for index in of_level(0):
-            plane_message(slot, index).start()
-        for row in range(2):
-            for side in range(2):
-                halo(slot, row, side).start()
+            if messages[index][2] == row:
+                plane_message(slot, index).start()
+
+    def send_halo(slot, row):
+        for side in range(2):
+            halo(slot, row, side).start()
 
     def pick(values, digit):
         out = values[0]
@@ -152,6 +151,8 @@
                     ifs[slot, level + 1, row] = near[row]
                 for index in of_level(level + 1):
                     plane_message(slot, index).start()
+            if level == max(0, len(levels) - 2):
+                send_halo(slot, 1)
             else:
                 far = [pick(got[row][1 : radix + 1], digit) for row in range(2)]
         used = 5 * cells
@@ -170,7 +171,7 @@
     is_first = small == 0
     is_last = small == width - 1
 
-    def layer(slot, new, row, t, k):
+    def layer(slot, new, row, t, k, ghosted):
         half_u = scal_ref[row, 0] * (0.5 * k)
         half_v = scal_ref[row, 1] * (0.5 * k)
         push_rho = scal_ref[row, 2] * (0.5 * k)
@@ -181,7 +182,7 @@
             r0 = pl.multiple_of(i * CHUNK, CHUNK)
             ke = eddy_ref[row, t - 1, pl.ds(r0, CHUNK), :] * k
             cf = ke * 6.0 + (1.5 / PHYS_STEP) * k
-            columns = gcol[pl.ds(r0, CHUNK), :]
+            columns = gcol[pl.ds(r0, CHUNK), :] if ghosted else None
             partial = []
             extra = {}
             div = None
@@ -196,11 +197,11 @@
                 j = row * block + (t - 1) * 5 + c
                 if row == 0:
                     am = jnp.where(is_first, 0.0, am)
-                    ap = jnp.where(is_last, pltpu.roll(columns, width - 1 - j, 1), ap)
+                    ghost = pltpu.roll(columns, width - 1 - j, 1) if ghosted else 0.0
+                    ap = jnp.where(is_last, ghost, ap)
                 else:
-                    am = jnp.where(
-                        is_first, pltpu.roll(columns, (width - j) % width, 1), am
-                    )
+                    ghost = pltpu.roll(columns, (width - j) % width, 1) if ghosted else 0.0
+                    am = jnp.where(is_first, ghost, am)
                     ap = jnp.where(is_last, f, ap)
                 da = ap - am
                 dt = tp - tm
@@ -233,6 +234,39 @@
             return carry
 
         lax.fori_loop(0, radial // CHUNK, body, 0)
+        if ghosted:
+            ghosts(new, row, t)
+
+    def patch(new, row, t, k):
+        sign = 1.0 if row == 0 else -1.0
+        half_u = scal_ref[row, 0] * (0.5 * sign * k)
+        push_rho = scal_ref[row, 2] * (0.5 * sign * k)
+        push_inv = scal_ref[row, 3] * (0.5 * sign * k)
+        push_p = scal_ref[row, 4] * (0.5 * sign * k)
+        here = is_last if row == 0 else is_first
+        edge = width - 1 if row == 0 else 0
+
+        def body(i, carry):
+            r0 = pl.multiple_of(i * CHUNK, CHUNK)
+            scale = eddy_ref[row, t - 1, pl.ds(r0, CHUNK), :] * k - half_u
+            columns = gcol[pl.ds(r0, CHUNK), :]
+            ghost = []
+            for c in range(5):
+                j = row * block + (t - 1) * 5 + c
+                ghost.append(jnp.where(here, pltpu.roll(columns, (edge - j) % width, 1), 0.0))
+            for c in range(5):
+                delta = scale * ghost[c]
+                if c == 0:
+                    delta = delta - push_rho * ghost[1]
+                elif c == 1:
+                    delta = delta - push_inv * ghost[4]
+                elif c == 4:
+                    delta = delta - push_p * ghost[1]
+                where = (new, c, row, t, pl.ds(r0 + PAD, CHUNK))
+                fbuf[where] = fbuf[where] + delta
+            return carry
+
+        lax.fori_loop(0, radial // CHUNK, body, 0)
         ghosts(new, row, t)
 
     for load in loads:
@@ -240,7 +274,10 @@
     for row in range(2):
         for t in range(cells):
             ghosts(0, row, t + 1)
-    publish(0)
+    for row in range(2):
+        pack(0, row, range(1, cells + 1), True)
+        send_plane(0, row)
+    send_halo(0, 0)
 
     def prepare(t, carry):
         for c in range(5):
@@ -271,10 +308,15 @@
 
             lax.fori_loop(0, cells, keep, 0)
 
+        inner = range(2, cells)
+        for row in range(2):
+            for t in inner:
+                layer(slot, new, row, t, k, False)
         interface(slot)
         for row in range(2):
-            for t in range(2, cells):
-                layer(slot, new, row, t, k)
+            for t in inner:
+                patch(new, row, t, k)
+            pack(new, row, inner, True)
 
         @pl.when(s > 0)
         def _():
@@ -286,14 +328,17 @@
             halo(slot, row, 1).wait_recv()
             if cells == 1:
                 halo(slot, row, 0).wait_recv()
-            layer(slot, new, row, 1, k)
+            layer(slot, new, row, 1, k, True)
             if cells > 1:
                 halo(slot, row, 0).wait_recv()
-                layer(slot, new, row, cells, k)
-
-        @pl.when(s < total - 1)
-        def _():
-            publish(new)
+                layer(slot, new, row, cells, k, True)
+
+            @pl.when(s < total - 1)
+            def _():
+                pack(new, row, sorted({1, cells}), False)
+                send_plane(new, row)
+                if row == 0:
+                    send_halo(new, 0)
 
         return carry
 
@@ -346,6 +391,7 @@
             pltpu.VMEM((5, 2, cells, radial, width), f32),
             pltpu.VMEM((5, 2, cells, radial, width), f32),
             pltpu.VMEM((radial, width), f32),
+            pltpu.VMEM((2, radial, width), f32),
             pltpu.VMEM((2, len(levels), 2, block, radial), f32),
             pltpu.VMEM((2, len(messages), block, radial), f32),
             pltpu.SemaphoreType.DMA((3,)),

time: 152 us -> 113 us (0.74)
  Pallas kernels: 145 us -> 105 us
    pallas_call x1, Pallas kernels: 145 us -> 105 us  [per_device(): pl.pallas_call(functools.partial(kernel, count, cells, radial), out_shape...]
where the time goes in v2:
time: 113 us; the launch traced here: 112 us
  Pallas kernels  105 us (93%)
  local copies, waits for them, and re-layouts  4.28 us (4%)
  other arithmetic  1.66 us (1%)
    pallas_call x1, Pallas kernels, per_device(): pl.pallas_call(functools.partial(kernel, count, cells, radial), out_shape...  105 us
    unnamed x5, local copies, waits for them, and re-layouts  4.28 us

profile of v2, /device:TPU:0, one launch (start us, length us, event | category | flops | bytes accessed | tf_op | source)
XLA Modules:
  0.0 111.8 jit_solution(6065323014923341344)
XLA Ops:
  0.7 0.1 pad_add_fusion.digit_ref
  0.8 0.8 slice_divide_fusion
  1.6 0.8 pad_maximum_fusion.scal_ref
  2.4 0.0 copy-start
  2.4 1.7 %copy-done = f32[5,2,4,128,128]{4,3,2,1,0:T(8,128)S(1)} copy-done((f32[5,2,4,128,128]{4,3,2,1,0:T(8,128)S(1)}, f32[5,2,4,128,128]{4,3,2,1,0:T(8,128)}, u32[]{:S(2)}) %copy-start) | copy-done | bytes 2621464
  4.1 0.0 copy-start.1
  4.1 1.0 copy-done.1
  5.2 105.2 %shard_map.55 = f32[5,2,4,128,128]{4,3,2,1,0:T(8,128)S(1)} custom-call(f32[2,5]{1,0:T(2,128)S(1)} %pad_maximum_fusion.scal_ref, s32[3]{0:T(128)S(1)} %pad_add_fusion.digit_ref, f32[5,2,4,128,128]{4,3,2,1,0:T(8,128)S(1)} %copy-done, f32[5,2,4,128,128]{4,3,2,1,0:T(8,128)} %prev_ref.1, f32[2,4,128,128]{3,2,1,0:T(8,128)S(1)} %copy-done.1), custom_call_target="tpu_custom_call" | custom-call | tf_op jit(solution)/shard_map/pallas_call | solution.py:378
  110.3 1.5 %copy.8 = f32[5,2,4,128,128]{4,3,2,1,0:T(8,128)} copy(f32[5,2,4,128,128]{4,3,2,1,0:T(8,128)S(1)} %shard_map.55) | data formatting | bytes 5242880
Async XLA Ops:
  2.4 1.7 %copy-start = (f32[5,2,4,128,128]{4,3,2,1,0:T(8,128)S(1)}, f32[5,2,4,128,128]{4,3,2,1,0:T(8,128)}, u32[]{:S(2)}) copy-start(f32[5,2,4,128,128]{4,3,2,1,0:T(8,128)} %now_ref.1) | copy-start | bytes 7864324
  4.1 1.0 copy-start.1

commit v3 on v2

--- a/solution.py
+++ b/solution.py
@@ -14,6 +14,7 @@
 WEIGHT_LAST = 1.0
 PAD = 8
 CHUNK = 64
+FIRST = (2, 1)
 
 
 def exchange_levels(count):
@@ -73,13 +74,14 @@
         )
     pl.semaphore_wait(barrier, len(reach))
 
-    def halo(slot, row, side):
+    def halo(slot, row, side, piece=0):
+        part = pl.ds(0, FIRST[row]) if piece == 0 else pl.ds(FIRST[row], 5 - FIRST[row])
         source, target = (1, cells + 1) if side == 0 else (cells, 0)
         return pltpu.make_async_remote_copy(
-            src_ref=fbuf.at[slot, :, row, source, pl.ds(PAD, radial)],
-            dst_ref=fbuf.at[slot, :, row, target, pl.ds(PAD, radial)],
-            send_sem=hsend.at[slot, row, side],
-            recv_sem=hrecv.at[slot, row, side],
+            src_ref=fbuf.at[slot, part, row, source, pl.ds(PAD, radial)],
+            dst_ref=fbuf.at[slot, part, row, target, pl.ds(PAD, radial)],
+            send_sem=hsend.at[slot, row, side, piece],
+            recv_sem=hrecv.at[slot, row, side, piece],
             device_id=peer(-1 if side == 0 else 1),
             device_id_type=pl.DeviceIdType.MESH,
         )
@@ -126,9 +128,18 @@
             if messages[index][2] == row:
                 plane_message(slot, index).start()
 
-    def send_halo(slot, row):
-        for side in range(2):
-            halo(slot, row, side).start()
+    def send_halo(slot, row, pieces=(0, 1)):
+        for piece in pieces:
+            for side in range(2):
+                halo(slot, row, side, piece).start()
+
+    def halo_wait_send(slot, row, side):
+        for piece in range(2):
+            halo(slot, row, side, piece).wait_send()
+
+    def halo_wait_recv(slot, row, side):
+        for piece in range(2):
+            halo(slot, row, side, piece).wait_recv()
 
     def pick(values, digit):
         out = values[0]
@@ -152,7 +163,7 @@
                 for index in of_level(level + 1):
                     plane_message(slot, index).start()
             if level == max(0, len(levels) - 2):
-                send_halo(slot, 1)
+                send_halo(slot, 1, (1,))
             else:
                 far = [pick(got[row][1 : radix + 1], digit) for row in range(2)]
         used = 5 * cells
@@ -269,15 +280,16 @@
         lax.fori_loop(0, radial // CHUNK, body, 0)
         ghosts(new, row, t)
 
-    for load in loads:
-        load.wait()
+    loads[0].wait()
+    send_halo(0, 0)
+    for row in range(2):
+        pack(0, row, range(1, cells + 1), True)
+        send_plane(0, row)
     for row in range(2):
         for t in range(cells):
             ghosts(0, row, t + 1)
-    for row in range(2):
-        pack(0, row, range(1, cells + 1), True)
-        send_plane(0, row)
-    send_halo(0, 0)
+    for load in loads[1:]:
+        load.wait()
 
     def prepare(t, carry):
         for c in range(5):
@@ -309,43 +321,53 @@
             lax.fori_loop(0, cells, keep, 0)
 
         inner = range(2, cells)
+        send_halo(slot, 1, (0,))
         for row in range(2):
             for t in inner:
                 layer(slot, new, row, t, k, False)
         interface(slot)
-        for row in range(2):
-            for t in inner:
-                patch(new, row, t, k)
-            pack(new, row, inner, True)
 
         @pl.when(s > 0)
         def _():
             for row in range(2):
                 for side in range(2):
-                    halo(new, row, side).wait_send()
+                    halo_wait_send(new, row, side)
 
         for row in range(2):
-            halo(slot, row, 1).wait_recv()
+            if row == 1:
+                for t in inner:
+                    patch(new, row, t, k)
+                pack(new, row, inner, True)
+            halo_wait_recv(slot, row, 1)
             if cells == 1:
-                halo(slot, row, 0).wait_recv()
+                halo_wait_recv(slot, row, 0)
             layer(slot, new, row, 1, k, True)
             if cells > 1:
-                halo(slot, row, 0).wait_recv()
+                halo_wait_recv(slot, row, 0)
                 layer(slot, new, row, cells, k, True)
+            if row == 0:
+
+                @pl.when(s < total - 1)
+                def _():
+                    send_halo(new, 0, (0,))
+
+                for t in inner:
+                    patch(new, row, t, k)
+                pack(new, row, inner, True)
 
             @pl.when(s < total - 1)
             def _():
                 pack(new, row, sorted({1, cells}), False)
                 send_plane(new, row)
                 if row == 0:
-                    send_halo(new, 0)
+                    send_halo(new, 0, (1,))
 
         return carry
 
     lax.fori_loop(0, total, section, 0)
     for row in range(2):
         for side in range(2):
-            halo((total - 1) % 2, row, side).wait_send()
+            halo_wait_send((total - 1) % 2, row, side)
     store = pltpu.make_async_copy(
         fbuf.at[total % 2, :, :, pl.ds(1, cells), pl.ds(PAD, radial)], out_ref, load_sem.at[0]
     )
@@ -395,8 +417,8 @@
             pltpu.VMEM((2, len(levels), 2, block, radial), f32),
             pltpu.VMEM((2, len(messages), block, radial), f32),
             pltpu.SemaphoreType.DMA((3,)),
-            pltpu.SemaphoreType.DMA((2, 2, 2)),
-            pltpu.SemaphoreType.DMA((2, 2, 2)),
+            pltpu.SemaphoreType.DMA((2, 2, 2, 2)),
+            pltpu.SemaphoreType.DMA((2, 2, 2, 2)),
             pltpu.SemaphoreType.DMA((2, len(messages))),
             pltpu.SemaphoreType.DMA((2, len(messages))),
         ],

time: 113 us -> 110 us (0.973)
  Pallas kernels: 105 us -> 103 us
    pallas_call x1, Pallas kernels: 105 us -> 103 us  [per_device(): pl.pallas_call(functools.partial(kernel, count, cells, radial), out_shape...]
where the time goes in v3:
time: 110 us; the launch traced here: 109 us
  Pallas kernels  103 us (94%)
  local copies, waits for them, and re-layouts  4.28 us (4%)
  other arithmetic  1.66 us (2%)
    pallas_call x1, Pallas kernels, per_device(): pl.pallas_call(functools.partial(kernel, count, cells, radial), out_shape...  103 us
    unnamed x5, local copies, waits for them, and re-layouts  4.28 us

profile of v3, /device:TPU:0, one launch (start us, length us, event | category | flops | bytes accessed | tf_op | source)
XLA Modules:
  0.0 109.4 jit_solution(9769018157543961049)
XLA Ops:
  0.7 0.1 pad_add_fusion.digit_ref
  0.8 0.8 slice_divide_fusion
  1.6 0.8 pad_maximum_fusion.scal_ref
  2.4 0.0 copy-start
  2.4 1.7 %copy-done = f32[5,2,4,128,128]{4,3,2,1,0:T(8,128)S(1)} copy-done((f32[5,2,4,128,128]{4,3,2,1,0:T(8,128)S(1)}, f32[5,2,4,128,128]{4,3,2,1,0:T(8,128)}, u32[]{:S(2)}) %copy-start) | copy-done | bytes 2621464
  4.1 0.0 copy-start.1
  4.1 1.0 copy-done.1
  5.2 102.7 %shard_map.55 = f32[5,2,4,128,128]{4,3,2,1,0:T(8,128)S(1)} custom-call(f32[2,5]{1,0:T(2,128)S(1)} %pad_maximum_fusion.scal_ref, s32[3]{0:T(128)S(1)} %pad_add_fusion.digit_ref, f32[5,2,4,128,128]{4,3,2,1,0:T(8,128)S(1)} %copy-done, f32[5,2,4,128,128]{4,3,2,1,0:T(8,128)} %prev_ref.1, f32[2,4,128,128]{3,2,1,0:T(8,128)S(1)} %copy-done.1), custom_call_target="tpu_custom_call" | custom-call | tf_op jit(solution)/shard_map/pallas_call | solution.py:400
  107.9 1.5 %copy.8 = f32[5,2,4,128,128]{4,3,2,1,0:T(8,128)} copy(f32[5,2,4,128,128]{4,3,2,1,0:T(8,128)S(1)} %shard_map.55) | data formatting | bytes 5242880
Async XLA Ops:
  2.4 1.7 %copy-start = (f32[5,2,4,128,128]{4,3,2,1,0:T(8,128)S(1)}, f32[5,2,4,128,128]{4,3,2,1,0:T(8,128)}, u32[]{:S(2)}) copy-start(f32[5,2,4,128,128]{4,3,2,1,0:T(8,128)} %now_ref.1) | copy-start | bytes 7864324
  4.1 1.0 copy-start.1

commit v4 on v3

--- a/solution.py
+++ b/solution.py
@@ -14,7 +14,7 @@
 WEIGHT_LAST = 1.0
 PAD = 8
 CHUNK = 64
-FIRST = (2, 1)
+FIRST = (3, 1)
 
 
 def exchange_levels(count):

time: 110 us -> 110 us (level)
  no operation moved by 1% of the time
where the time goes in v4:
time: 110 us
  Pallas kernels  103 us (94%)
  local copies, waits for them, and re-layouts  4.28 us (4%)
  other arithmetic  1.66 us (2%)
    pallas_call x1, Pallas kernels, per_device(): pl.pallas_call(functools.partial(kernel, count, cells, radial), out_shape...  103 us
    unnamed x5, local copies, waits for them, and re-layouts  4.28 us

profile of v4, /device:TPU:0, one launch (start us, length us, event | category | flops | bytes accessed | tf_op | source)
XLA Modules:
  0.0 109.6 jit_solution(4196116991314367243)
XLA Ops:
  0.7 0.1 pad_add_fusion.digit_ref
  0.8 0.8 slice_divide_fusion
  1.6 0.8 pad_maximum_fusion.scal_ref
  2.4 0.0 copy-start
  2.4 1.7 %copy-done = f32[5,2,4,128,128]{4,3,2,1,0:T(8,128)S(1)} copy-done((f32[5,2,4,128,128]{4,3,2,1,0:T(8,128)S(1)}, f32[5,2,4,128,128]{4,3,2,1,0:T(8,128)}, u32[]{:S(2)}) %copy-start) | copy-done | bytes 2621464
  4.1 0.0 copy-start.1
  4.1 1.0 copy-done.1
  5.2 102.9 %shard_map.55 = f32[5,2,4,128,128]{4,3,2,1,0:T(8,128)S(1)} custom-call(f32[2,5]{1,0:T(2,128)S(1)} %pad_maximum_fusion.scal_ref, s32[3]{0:T(128)S(1)} %pad_add_fusion.digit_ref, f32[5,2,4,128,128]{4,3,2,1,0:T(8,128)S(1)} %copy-done, f32[5,2,4,128,128]{4,3,2,1,0:T(8,128)} %prev_ref.1, f32[2,4,128,128]{3,2,1,0:T(8,128)S(1)} %copy-done.1), custom_call_target="tpu_custom_call" | custom-call | tf_op jit(solution)/shard_map/pallas_call | solution.py:400
  108.1 1.5 %copy.8 = f32[5,2,4,128,128]{4,3,2,1,0:T(8,128)} copy(f32[5,2,4,128,128]{4,3,2,1,0:T(8,128)S(1)} %shard_map.55) | data formatting | bytes 5242880
Async XLA Ops:
  2.4 1.7 %copy-start = (f32[5,2,4,128,128]{4,3,2,1,0:T(8,128)S(1)}, f32[5,2,4,128,128]{4,3,2,1,0:T(8,128)}, u32[]{:S(2)}) copy-start(f32[5,2,4,128,128]{4,3,2,1,0:T(8,128)} %now_ref.1) | copy-start | bytes 7864324
  4.1 1.0 copy-start.1
